TPU v7x, 128 devices: a whole 4x4x4 slice. The times are simulated.
128 devices in a mesh: section: 8 (over x, core), tp: 16 (over z, y).
Axes of the slice: x: 4, y: 4, z: 4, core: 2. Of those that a mesh axis runs over, the one named last changes fastest.
Arguments:
- layer_inputs: bfloat16 [16, 512, 4096], P('section', None, 'tp'), may hold values from -6 to 6
- weights: bfloat16 [16, 4096, 4096], P('section', 'tp'), may hold values from -0.046875 to 0.046875
- input_basis: bfloat16 [16, 4096, 64], P('section', 'tp'), may hold values from -0.09375 to 0.09375
- output_basis: bfloat16 [16, 4096, 32], P('section', 'tp'), may hold values from -0.09375 to 0.09375
- queries: bfloat16 [16, 512, 2048], P('section', 'tp'), may hold values from -0.00390625 to 0.00390625
- top_cotangent: bfloat16 [512, 4096], replicated, may hold values from -6 to 6
- sequence_example: int32 [4], replicated, may hold values from 0 to 1
Outputs:
- scores: float32 [2, 512], P(None, 'tp')
All inputs are finite; a program needn't handle non-finite values.
Results may differ from a plain program's by a relative error of at most 0.0094.
Values may be sent and summed in bfloat16 or wider, within the bound.
No kernel may reach another device: no remote copies, remote signals or barrier semaphores. Data moves between devices by JAX's collectives and lax.ppermute only.
A program may use at most 64 MiB of HBM per device.

v0:
```python
import jax
import jax.numpy as jnp
from jax import lax
from jax.sharding import PartitionSpec as P

SEQLEN = 128
SEQ_MB = 1
MB = 4
EXAMPLES = 2


def from_behind(value, axis, by):
    size = lax.axis_size(axis)
    pairs = [(i, i + by) for i in range(size) if 0 <= i + by < size]
    return lax.ppermute(value, axis, pairs)


def silu_parts(values):
    floats = values.astype(jnp.float32)
    logistic = jax.nn.sigmoid(floats)
    return ((floats * logistic).astype(jnp.bfloat16), logistic * (1.0 + floats * (1.0 - logistic)))


def contract_columns(portion, matrix):
    return lax.dot_general(
        portion, matrix, (((1,), (1,)), ((), ())), preferred_element_type=jnp.float32
    )


def outer_rows(out_feats, in_feats):
    joined = out_feats[:, :, :, None] * in_feats[:, :, None, :]
    return joined.reshape(joined.shape[0], joined.shape[1], -1)


def shards(
    layer_inputs, weights, input_basis, output_basis, queries, top_cotangent, sequence_example
):
    section_count = lax.axis_size("section")
    section_rank = lax.axis_index("section")
    tp_rank = lax.axis_index("tp")
    width_local = layer_inputs.shape[2]
    width_full = weights.shape[2]
    total_tokens = layer_inputs.shape[1]
    block_rows = SEQ_MB * SEQLEN
    activated, slopes = silu_parts(layer_inputs)
    partial_in = jnp.einsum(
        "ltd,ldr->tlr", activated, input_basis, preferred_element_type=jnp.float32
    )
    in_feats = lax.psum(partial_in.reshape(total_tokens, -1), "tp").reshape(partial_in.shape)
    example_index = jnp.arange(EXAMPLES, dtype=jnp.int32)
    is_top = section_rank == section_count - 1

    def fold_lower(portion):
        return contract_columns(portion, weights[0])

    def tick(tick_index, state):
        outgoing, grads, stored = state
        micro_index = tick_index - (section_count - 1 - section_rank)
        valid = (micro_index >= 0) & (micro_index < MB)
        micro_clip = jnp.clip(micro_index, 0, MB - 1)
        first_row = micro_clip * block_rows
        slope_block = lax.dynamic_slice_in_dim(slopes, first_row, block_rows, 1)
        received = from_behind(outgoing, "section", -1)
        top_block = lax.dynamic_slice_in_dim(top_cotangent, first_row, block_rows, 0)
        upper_full = jnp.where(is_top, top_block, received)
        upper_own = lax.dynamic_slice_in_dim(upper_full, tp_rank * width_local, width_local, 1)
        upper_branch = lax.dot_general(
            upper_full, weights[1], (((1,), (1,)), ((), ())), preferred_element_type=jnp.float32
        )
        middle_own = (upper_own.astype(jnp.float32) + slope_block[1] * upper_branch).astype(
            jnp.bfloat16
        )
        lower_branch = fold_lower(lax.all_gather(middle_own, "tp", axis=1, tiled=True))
        lower_own = (middle_own.astype(jnp.float32) + slope_block[0] * lower_branch).astype(
            jnp.bfloat16
        )
        new_outgoing = lax.all_gather(lower_own, "tp", axis=1, tiled=True)
        cotangents = jnp.stack([middle_own, upper_own], 0)
        partial_out = jnp.einsum(
            "lrd,ldk->rlk", cotangents, output_basis, preferred_element_type=jnp.float32
        )
        out_feats = lax.psum(partial_out.reshape(block_rows, -1), "tp").reshape(partial_out.shape)
        in_block = lax.dynamic_slice_in_dim(in_feats, first_row, block_rows, 0)
        block_examples = jnp.repeat(
            lax.dynamic_slice_in_dim(sequence_example, micro_clip * SEQ_MB, SEQ_MB, 0), SEQLEN
        )
        selector = (example_index[:, None] == block_examples[None, :]).astype(
            jnp.float32
        ) * valid.astype(jnp.float32)
        grads = grads + jnp.einsum(
            "er,rlk->lek",
            selector,
            outer_rows(out_feats, in_block),
            precision=lax.Precision.HIGHEST,
        )
        return (new_outgoing, grads, stored)

    outgoing_init = jnp.zeros((block_rows, width_full), jnp.bfloat16)
    grads_init = jnp.zeros((2, EXAMPLES, queries.shape[2]), jnp.float32)
    stored_init = jnp.zeros((1,), jnp.bfloat16)
    final_out, grads, stored = lax.fori_loop(
        0, MB + section_count - 1, tick, (outgoing_init, grads_init, stored_init)
    )
    layer_scores = jnp.einsum(
        "lek,lqk->eq", grads, queries.astype(jnp.float32), precision=lax.Precision.HIGHEST
    )
    return lax.psum(layer_scores, "section")


def solution(mesh):
    placed = (
        P("section", None, "tp"),
        P("section", "tp", None),
        P("section", "tp", None),
        P("section", "tp", None),
        P("section", "tp", None),
        P(),
        P(),
    )
    return jax.shard_map(
        shards, mesh=mesh, in_specs=placed, out_specs=P(None, "tp"), check_vma=False
    )
```

profile of v0, /device:TPU:1, one launch (start us, length us, event | category | flops | bytes accessed | tf_op | source)
XLA Modules:
  0.0 1662.4 jit_solution(13824720775074881913)
XLA Ops:
  9.2 87.7 %all-reduce.2.cloned.1.call-done = f32[512,2,64]{0,2,1:T(8,128)} async-done(((f32[512,2,64]{0,2,1:T(8,128)}), f32[512,2,64]{0,2,1:T(8,128)}) %all-reduce.2.cloned.1.call-update) | async-done | bytes 262160 | tf_op jit(solution)/shard_map/psum | solution.py:49
  98.0 1529.4 %while.18 = (s32[]{:T(128)}, bf16[128,4096]{1,0:T(8,128)(2,1)}, f32[2,2,2048]{2,1,0:T(2,128)S(1)}, pred[]{:T(512)}, s32[]{:T(128)}, /*index=5*/bf16[512,4096]{1,...) while((s32[]{:T(128)}, bf16[128,4096]{1,0:T(8,128)(2,1)}, ...), condition=%wide.region_3.4_spmd.clone, body=%wide.region_1.3_spmd.clone.sunk | while | flops 555048960 | bytes 25986044 | solution.py:101
  98.0 3.9 collective-permute-start
  101.9 13.7 collective-permute-done
  120.3 40.6 %all-gather.3.cloned.1.call-done = bf16[128,4096]{1,0:T(8,128)(2,1)} async-done(((bf16[128,256]{1,0:T(8,128)(2,1)}), bf16[128,4096]{1,0:T(8,128)(2,1)}) %all-gather.3.cloned.1.call-update) | async-done | bytes 1048592 | tf_op jit(solution)/shard_map/while/body/eval_jaxpr/all_gather | solution.py:73
  160.9 3.3 add_convert_fusion.5
  166.6 58.4 %psum.31 = f32[128,2,32]{0,2,1:T(8,128)S(1)} all-reduce(f32[128,2,32]{0,2,1:T(8,128)S(1)} %convolution_bitcast_fusion.5), channel_id=1, replica_groups=mesh['section'=8,'tp'=16] {'tp'}, use_global_device_ids=true, to_apply=%region_2.2 | all-reduce | flops 8192 | bytes 65536 | tf_op jit(solution)/shard_map/while/body/eval_jaxpr/psum | solution.py:82
  227.2 17.7 %collective-permute-start = (bf16[128,4096]{1,0:T(8,128)(2,1)}, bf16[128,4096]{1,0:T(8,128)(2,1)S(1)}, u32[]{:S(2)}, u32[]{:S(2)}) collective-permute-start(bf16[128,4096]{1,0:T(8,128)(2,1)} %get-tuple-element.465), channel_id=1, source_target_pairs={{16,0},{32,16},{48,32},{64,48},{80,64},{96,80},{112,96},{17,1},{33... | collective-permute-start | bytes 3145736 | tf_op jit(solution)/shard_map/while/body/eval_jaxpr/ppermute | solution.py:15
  244.9 13.7 collective-permute-done
  263.3 37.6 %all-gather.3.cloned.1.call-done = bf16[128,4096]{1,0:T(8,128)(2,1)} async-done(((bf16[128,256]{1,0:T(8,128)(2,1)}), bf16[128,4096]{1,0:T(8,128)(2,1)}) %all-gather.3.cloned.1.call-update) | async-done | bytes 1048592 | tf_op jit(solution)/shard_map/while/body/eval_jaxpr/all_gather | solution.py:73
  306.6 58.4 %psum.31 = f32[128,2,32]{0,2,1:T(8,128)S(1)} all-reduce(f32[128,2,32]{0,2,1:T(8,128)S(1)} %convolution_bitcast_fusion.5), channel_id=1, replica_groups=mesh['section'=8,'tp'=16] {'tp'}, use_global_device_ids=true, to_apply=%region_2.2 | all-reduce | flops 8192 | bytes 65536 | tf_op jit(solution)/shard_map/while/body/eval_jaxpr/psum | solution.py:82
  367.3 17.7 %collective-permute-start = (bf16[128,4096]{1,0:T(8,128)(2,1)}, bf16[128,4096]{1,0:T(8,128)(2,1)S(1)}, u32[]{:S(2)}, u32[]{:S(2)}) collective-permute-start(bf16[128,4096]{1,0:T(8,128)(2,1)} %get-tuple-element.465), channel_id=1, source_target_pairs={{16,0},{32,16},{48,32},{64,48},{80,64},{96,80},{112,96},{17,1},{33... | collective-permute-start | bytes 3145736 | tf_op jit(solution)/shard_map/while/body/eval_jaxpr/ppermute | solution.py:15
  385.0 13.7 collective-permute-done
  403.3 37.6 %all-gather.3.cloned.1.call-done = bf16[128,4096]{1,0:T(8,128)(2,1)} async-done(((bf16[128,256]{1,0:T(8,128)(2,1)}), bf16[128,4096]{1,0:T(8,128)(2,1)}) %all-gather.3.cloned.1.call-update) | async-done | bytes 1048592 | tf_op jit(solution)/shard_map/while/body/eval_jaxpr/all_gather | solution.py:73
  446.6 58.4 %psum.31 = f32[128,2,32]{0,2,1:T(8,128)S(1)} all-reduce(f32[128,2,32]{0,2,1:T(8,128)S(1)} %convolution_bitcast_fusion.5), channel_id=1, replica_groups=mesh['section'=8,'tp'=16] {'tp'}, use_global_device_ids=true, to_apply=%region_2.2 | all-reduce | flops 8192 | bytes 65536 | tf_op jit(solution)/shard_map/while/body/eval_jaxpr/psum | solution.py:82
  507.3 17.7 %collective-permute-start = (bf16[128,4096]{1,0:T(8,128)(2,1)}, bf16[128,4096]{1,0:T(8,128)(2,1)S(1)}, u32[]{:S(2)}, u32[]{:S(2)}) collective-permute-start(bf16[128,4096]{1,0:T(8,128)(2,1)} %get-tuple-element.465), channel_id=1, source_target_pairs={{16,0},{32,16},{48,32},{64,48},{80,64},{96,80},{112,96},{17,1},{33... | collective-permute-start | bytes 3145736 | tf_op jit(solution)/shard_map/while/body/eval_jaxpr/ppermute | solution.py:15
  525.0 13.7 collective-permute-done
  543.4 37.6 %all-gather.3.cloned.1.call-done = bf16[128,4096]{1,0:T(8,128)(2,1)} async-done(((bf16[128,256]{1,0:T(8,128)(2,1)}), bf16[128,4096]{1,0:T(8,128)(2,1)}) %all-gather.3.cloned.1.call-update) | async-done | bytes 1048592 | tf_op jit(solution)/shard_map/while/body/eval_jaxpr/all_gather | solution.py:73
  586.7 58.4 %psum.31 = f32[128,2,32]{0,2,1:T(8,128)S(1)} all-reduce(f32[128,2,32]{0,2,1:T(8,128)S(1)} %convolution_bitcast_fusion.5), channel_id=1, replica_groups=mesh['section'=8,'tp'=16] {'tp'}, use_global_device_ids=true, to_apply=%region_2.2 | all-reduce | flops 8192 | bytes 65536 | tf_op jit(solution)/shard_map/while/body/eval_jaxpr/psum | solution.py:82
  647.3 17.7 %collective-permute-start = (bf16[128,4096]{1,0:T(8,128)(2,1)}, bf16[128,4096]{1,0:T(8,128)(2,1)S(1)}, u32[]{:S(2)}, u32[]{:S(2)}) collective-permute-start(bf16[128,4096]{1,0:T(8,128)(2,1)} %get-tuple-element.465), channel_id=1, source_target_pairs={{16,0},{32,16},{48,32},{64,48},{80,64},{96,80},{112,96},{17,1},{33... | collective-permute-start | bytes 3145736 | tf_op jit(solution)/shard_map/while/body/eval_jaxpr/ppermute | solution.py:15
  665.0 13.7 collective-permute-done
  683.4 37.6 %all-gather.3.cloned.1.call-done = bf16[128,4096]{1,0:T(8,128)(2,1)} async-done(((bf16[128,256]{1,0:T(8,128)(2,1)}), bf16[128,4096]{1,0:T(8,128)(2,1)}) %all-gather.3.cloned.1.call-update) | async-done | bytes 1048592 | tf_op jit(solution)/shard_map/while/body/eval_jaxpr/all_gather | solution.py:73
  726.7 58.4 %psum.31 = f32[128,2,32]{0,2,1:T(8,128)S(1)} all-reduce(f32[128,2,32]{0,2,1:T(8,128)S(1)} %convolution_bitcast_fusion.5), channel_id=1, replica_groups=mesh['section'=8,'tp'=16] {'tp'}, use_global_device_ids=true, to_apply=%region_2.2 | all-reduce | flops 8192 | bytes 65536 | tf_op jit(solution)/shard_map/while/body/eval_jaxpr/psum | solution.py:82
  787.3 17.7 %collective-permute-start = (bf16[128,4096]{1,0:T(8,128)(2,1)}, bf16[128,4096]{1,0:T(8,128)(2,1)S(1)}, u32[]{:S(2)}, u32[]{:S(2)}) collective-permute-start(bf16[128,4096]{1,0:T(8,128)(2,1)} %get-tuple-element.465), channel_id=1, source_target_pairs={{16,0},{32,16},{48,32},{64,48},{80,64},{96,80},{112,96},{17,1},{33... | collective-permute-start | bytes 3145736 | tf_op jit(solution)/shard_map/while/body/eval_jaxpr/ppermute | solution.py:15
  805.0 13.7 collective-permute-done
  823.4 37.6 %all-gather.3.cloned.1.call-done = bf16[128,4096]{1,0:T(8,128)(2,1)} async-done(((bf16[128,256]{1,0:T(8,128)(2,1)}), bf16[128,4096]{1,0:T(8,128)(2,1)}) %all-gather.3.cloned.1.call-update) | async-done | bytes 1048592 | tf_op jit(solution)/shard_map/while/body/eval_jaxpr/all_gather | solution.py:73
  866.7 58.4 %psum.31 = f32[128,2,32]{0,2,1:T(8,128)S(1)} all-reduce(f32[128,2,32]{0,2,1:T(8,128)S(1)} %convolution_bitcast_fusion.5), channel_id=1, replica_groups=mesh['section'=8,'tp'=16] {'tp'}, use_global_device_ids=true, to_apply=%region_2.2 | all-reduce | flops 8192 | bytes 65536 | tf_op jit(solution)/shard_map/while/body/eval_jaxpr/psum | solution.py:82
  927.4 17.7 %collective-permute-start = (bf16[128,4096]{1,0:T(8,128)(2,1)}, bf16[128,4096]{1,0:T(8,128)(2,1)S(1)}, u32[]{:S(2)}, u32[]{:S(2)}) collective-permute-start(bf16[128,4096]{1,0:T(8,128)(2,1)} %get-tuple-element.465), channel_id=1, source_target_pairs={{16,0},{32,16},{48,32},{64,48},{80,64},{96,80},{112,96},{17,1},{33... | collective-permute-start | bytes 3145736 | tf_op jit(solution)/shard_map/while/body/eval_jaxpr/ppermute | solution.py:15
  945.1 13.7 collective-permute-done
  963.4 37.6 %all-gather.3.cloned.1.call-done = bf16[128,4096]{1,0:T(8,128)(2,1)} async-done(((bf16[128,256]{1,0:T(8,128)(2,1)}), bf16[128,4096]{1,0:T(8,128)(2,1)}) %all-gather.3.cloned.1.call-update) | async-done | bytes 1048592 | tf_op jit(solution)/shard_map/while/body/eval_jaxpr/all_gather | solution.py:73
  1006.7 58.4 %psum.31 = f32[128,2,32]{0,2,1:T(8,128)S(1)} all-reduce(f32[128,2,32]{0,2,1:T(8,128)S(1)} %convolution_bitcast_fusion.5), channel_id=1, replica_groups=mesh['section'=8,'tp'=16] {'tp'}, use_global_device_ids=true, to_apply=%region_2.2 | all-reduce | flops 8192 | bytes 65536 | tf_op jit(solution)/shard_map/while/body/eval_jaxpr/psum | solution.py:82
  1067.4 17.7 %collective-permute-start = (bf16[128,4096]{1,0:T(8,128)(2,1)}, bf16[128,4096]{1,0:T(8,128)(2,1)S(1)}, u32[]{:S(2)}, u32[]{:S(2)}) collective-permute-start(bf16[128,4096]{1,0:T(8,128)(2,1)} %get-tuple-element.465), channel_id=1, source_target_pairs={{16,0},{32,16},{48,32},{64,48},{80,64},{96,80},{112,96},{17,1},{33... | collective-permute-start | bytes 3145736 | tf_op jit(solution)/shard_map/while/body/eval_jaxpr/ppermute | solution.py:15
  1085.1 13.7 collective-permute-done
  1103.5 37.6 %all-gather.3.cloned.1.call-done = bf16[128,4096]{1,0:T(8,128)(2,1)} async-done(((bf16[128,256]{1,0:T(8,128)(2,1)}), bf16[128,4096]{1,0:T(8,128)(2,1)}) %all-gather.3.cloned.1.call-update) | async-done | bytes 1048592 | tf_op jit(solution)/shard_map/while/body/eval_jaxpr/all_gather | solution.py:73
  1146.8 58.4 %psum.31 = f32[128,2,32]{0,2,1:T(8,128)S(1)} all-reduce(f32[128,2,32]{0,2,1:T(8,128)S(1)} %convolution_bitcast_fusion.5), channel_id=1, replica_groups=mesh['section'=8,'tp'=16] {'tp'}, use_global_device_ids=true, to_apply=%region_2.2 | all-reduce | flops 8192 | bytes 65536 | tf_op jit(solution)/shard_map/while/body/eval_jaxpr/psum | solution.py:82
  1207.4 17.7 %collective-permute-start = (bf16[128,4096]{1,0:T(8,128)(2,1)}, bf16[128,4096]{1,0:T(8,128)(2,1)S(1)}, u32[]{:S(2)}, u32[]{:S(2)}) collective-permute-start(bf16[128,4096]{1,0:T(8,128)(2,1)} %get-tuple-element.465), channel_id=1, source_target_pairs={{16,0},{32,16},{48,32},{64,48},{80,64},{96,80},{112,96},{17,1},{33... | collective-permute-start | bytes 3145736 | tf_op jit(solution)/shard_map/while/body/eval_jaxpr/ppermute | solution.py:15
  1225.1 13.7 collective-permute-done
  1243.5 37.6 %all-gather.3.cloned.1.call-done = bf16[128,4096]{1,0:T(8,128)(2,1)} async-done(((bf16[128,256]{1,0:T(8,128)(2,1)}), bf16[128,4096]{1,0:T(8,128)(2,1)}) %all-gather.3.cloned.1.call-update) | async-done | bytes 1048592 | tf_op jit(solution)/shard_map/while/body/eval_jaxpr/all_gather | solution.py:73
  1286.8 58.4 %psum.31 = f32[128,2,32]{0,2,1:T(8,128)S(1)} all-reduce(f32[128,2,32]{0,2,1:T(8,128)S(1)} %convolution_bitcast_fusion.5), channel_id=1, replica_groups=mesh['section'=8,'tp'=16] {'tp'}, use_global_device_ids=true, to_apply=%region_2.2 | all-reduce | flops 8192 | bytes 65536 | tf_op jit(solution)/shard_map/while/body/eval_jaxpr/psum | solution.py:82
  1347.4 17.7 %collective-permute-start = (bf16[128,4096]{1,0:T(8,128)(2,1)}, bf16[128,4096]{1,0:T(8,128)(2,1)S(1)}, u32[]{:S(2)}, u32[]{:S(2)}) collective-permute-start(bf16[128,4096]{1,0:T(8,128)(2,1)} %get-tuple-element.465), channel_id=1, source_target_pairs={{16,0},{32,16},{48,32},{64,48},{80,64},{96,80},{112,96},{17,1},{33... | collective-permute-start | bytes 3145736 | tf_op jit(solution)/shard_map/while/body/eval_jaxpr/ppermute | solution.py:15
  1365.1 13.7 collective-permute-done
  1383.5 37.6 %all-gather.3.cloned.1.call-done = bf16[128,4096]{1,0:T(8,128)(2,1)} async-done(((bf16[128,256]{1,0:T(8,128)(2,1)}), bf16[128,4096]{1,0:T(8,128)(2,1)}) %all-gather.3.cloned.1.call-update) | async-done | bytes 1048592 | tf_op jit(solution)/shard_map/while/body/eval_jaxpr/all_gather | solution.py:73
  1426.8 58.4 %psum.31 = f32[128,2,32]{0,2,1:T(8,128)S(1)} all-reduce(f32[128,2,32]{0,2,1:T(8,128)S(1)} %convolution_bitcast_fusion.5), channel_id=1, replica_groups=mesh['section'=8,'tp'=16] {'tp'}, use_global_device_ids=true, to_apply=%region_2.2 | all-reduce | flops 8192 | bytes 65536 | tf_op jit(solution)/shard_map/while/body/eval_jaxpr/psum | solution.py:82
  1487.5 17.7 %collective-permute-start = (bf16[128,4096]{1,0:T(8,128)(2,1)}, bf16[128,4096]{1,0:T(8,128)(2,1)S(1)}, u32[]{:S(2)}, u32[]{:S(2)}) collective-permute-start(bf16[128,4096]{1,0:T(8,128)(2,1)} %get-tuple-element.465), channel_id=1, source_target_pairs={{16,0},{32,16},{48,32},{64,48},{80,64},{96,80},{112,96},{17,1},{33... | collective-permute-start | bytes 3145736 | tf_op jit(solution)/shard_map/while/body/eval_jaxpr/ppermute | solution.py:15
  1505.2 13.7 collective-permute-done
  1523.5 37.6 %all-gather.3.cloned.1.call-done = bf16[128,4096]{1,0:T(8,128)(2,1)} async-done(((bf16[128,256]{1,0:T(8,128)(2,1)}), bf16[128,4096]{1,0:T(8,128)(2,1)}) %all-gather.3.cloned.1.call-update) | async-done | bytes 1048592 | tf_op jit(solution)/shard_map/while/body/eval_jaxpr/all_gather | solution.py:73
  1566.8 58.4 %psum.31 = f32[128,2,32]{0,2,1:T(8,128)S(1)} all-reduce(f32[128,2,32]{0,2,1:T(8,128)S(1)} %convolution_bitcast_fusion.5), channel_id=1, replica_groups=mesh['section'=8,'tp'=16] {'tp'}, use_global_device_ids=true, to_apply=%region_2.2 | all-reduce | flops 8192 | bytes 65536 | tf_op jit(solution)/shard_map/while/body/eval_jaxpr/psum | solution.py:82
  1627.8 28.1 %psum.28 = f32[2,32]{1,0:T(2,128)} all-reduce(f32[2,32]{1,0:T(2,128)S(1)} %convolution_bitcast_fusion.3), channel_id=1, replica_groups=mesh['section'=8,'tp'=16] {'section'}, use_global_device_ids=true, to_apply=%region_4.5 | all-reduce | flops 64 | bytes 512 | tf_op jit(solution)/shard_map/psum | solution.py:107
  (201 shorter events, 137.2 us)
Async XLA Ops:
  6.5 1620.9 %copy-start = (bf16[2,32,2048]{2,1,0:T(8,128)(2,1)S(1)}, bf16[2,32,2048]{2,1,0:T(8,128)(2,1)}, u32[]{:S(2)}) copy-start(bf16[2,32,2048]{2,1,0:T(8,128)(2,1)} %param.13) | copy-start | bytes 786436
  6.5 90.4 %all-reduce.2.cloned.1.call-start = ((), (), s32[]{:S(2)}) async-start(), calls=%async_computation | async-start | bytes 524288 | tf_op jit(solution)/shard_map/psum | solution.py:49
  8.8 89.2 %copy-start.3 = (bf16[2,256,32]{1,2,0:T(8,128)(2,1)S(1)}, bf16[2,256,32]{1,2,0:T(8,128)(2,1)}, u32[]{:S(2)}) copy-start(bf16[2,256,32]{1,2,0:T(8,128)(2,1)} %param.12) | copy-start | bytes 98308
  8.8 89.2 %copy-start.4 = (s32[4]{0:T(128)S(1)}, s32[4]{0:T(128)}, u32[]{:S(2)}) copy-start(s32[4]{0:T(128)} %param.15) | copy-start | bytes 52
  98.0 62.9 %all-gather.3.cloned.1.call-start = ((), (), s32[]{:S(2)}) async-start(), calls=%async_computation.1 | async-start | bytes 1114112 | tf_op jit(solution)/shard_map/while/body/eval_jaxpr/all_gather | solution.py:73
  98.0 17.6 %collective-permute-start = (bf16[128,4096]{1,0:T(8,128)(2,1)}, bf16[128,4096]{1,0:T(8,128)(2,1)S(1)}, u32[]{:S(2)}, u32[]{:S(2)}) collective-permute-start(bf16[128,4096]{1,0:T(8,128)(2,1)} %get-tuple-element.465), channel_id=1, source_target_pairs={{16,0},{32,16},{48,32},{64,48},{80,64},{96,80},{112,96},{17,1},{33... | collective-permute-start | bytes 3145736 | tf_op jit(solution)/shard_map/while/body/eval_jaxpr/ppermute | solution.py:15
  120.2 46.2 %copy-start.1 = (bf16[128,256]{1,0:T(8,128)(2,1)S(1)}, bf16[128,256]{1,0:T(8,128)(2,1)}, u32[]{:S(2)}) copy-start(bf16[128,256]{1,0:T(8,128)(2,1)} %add_convert_fusion.4) | copy-start | bytes 196612 | tf_op jit(solution)/shard_map/while
  120.2 106.9 %all-gather.5.cloned.1.call-start = ((), (), s32[]{:S(2)}) async-start(), calls=%async_computation.2 | async-start | bytes 1114112 | tf_op jit(solution)/shard_map/while/body/eval_jaxpr/all_gather | solution.py:77
  227.2 73.7 %all-gather.3.cloned.1.call-start = ((), (), s32[]{:S(2)}) async-start(), calls=%async_computation.1 | async-start | bytes 1114112 | tf_op jit(solution)/shard_map/while/body/eval_jaxpr/all_gather | solution.py:73
  227.2 31.4 %collective-permute-start = (bf16[128,4096]{1,0:T(8,128)(2,1)}, bf16[128,4096]{1,0:T(8,128)(2,1)S(1)}, u32[]{:S(2)}, u32[]{:S(2)}) collective-permute-start(bf16[128,4096]{1,0:T(8,128)(2,1)} %get-tuple-element.465), channel_id=1, source_target_pairs={{16,0},{32,16},{48,32},{64,48},{80,64},{96,80},{112,96},{17,1},{33... | collective-permute-start | bytes 3145736 | tf_op jit(solution)/shard_map/while/body/eval_jaxpr/ppermute | solution.py:15
  263.2 43.2 %copy-start.1 = (bf16[128,256]{1,0:T(8,128)(2,1)S(1)}, bf16[128,256]{1,0:T(8,128)(2,1)}, u32[]{:S(2)}) copy-start(bf16[128,256]{1,0:T(8,128)(2,1)} %add_convert_fusion.4) | copy-start | bytes 196612 | tf_op jit(solution)/shard_map/while
  263.3 103.9 %all-gather.5.cloned.1.call-start = ((), (), s32[]{:S(2)}) async-start(), calls=%async_computation.2 | async-start | bytes 1114112 | tf_op jit(solution)/shard_map/while/body/eval_jaxpr/all_gather | solution.py:77
  367.2 73.8 %all-gather.3.cloned.1.call-start = ((), (), s32[]{:S(2)}) async-start(), calls=%async_computation.1 | async-start | bytes 1114112 | tf_op jit(solution)/shard_map/while/body/eval_jaxpr/all_gather | solution.py:73
  367.3 31.4 %collective-permute-start = (bf16[128,4096]{1,0:T(8,128)(2,1)}, bf16[128,4096]{1,0:T(8,128)(2,1)S(1)}, u32[]{:S(2)}, u32[]{:S(2)}) collective-permute-start(bf16[128,4096]{1,0:T(8,128)(2,1)} %get-tuple-element.465), channel_id=1, source_target_pairs={{16,0},{32,16},{48,32},{64,48},{80,64},{96,80},{112,96},{17,1},{33... | collective-permute-start | bytes 3145736 | tf_op jit(solution)/shard_map/while/body/eval_jaxpr/ppermute | solution.py:15
  403.3 43.2 %copy-start.1 = (bf16[128,256]{1,0:T(8,128)(2,1)S(1)}, bf16[128,256]{1,0:T(8,128)(2,1)}, u32[]{:S(2)}) copy-start(bf16[128,256]{1,0:T(8,128)(2,1)} %add_convert_fusion.4) | copy-start | bytes 196612 | tf_op jit(solution)/shard_map/while
  403.3 103.9 %all-gather.5.cloned.1.call-start = ((), (), s32[]{:S(2)}) async-start(), calls=%async_computation.2 | async-start | bytes 1114112 | tf_op jit(solution)/shard_map/while/body/eval_jaxpr/all_gather | solution.py:77
  507.2 73.8 %all-gather.3.cloned.1.call-start = ((), (), s32[]{:S(2)}) async-start(), calls=%async_computation.1 | async-start | bytes 1114112 | tf_op jit(solution)/shard_map/while/body/eval_jaxpr/all_gather | solution.py:73
  507.3 31.4 %collective-permute-start = (bf16[128,4096]{1,0:T(8,128)(2,1)}, bf16[128,4096]{1,0:T(8,128)(2,1)S(1)}, u32[]{:S(2)}, u32[]{:S(2)}) collective-permute-start(bf16[128,4096]{1,0:T(8,128)(2,1)} %get-tuple-element.465), channel_id=1, source_target_pairs={{16,0},{32,16},{48,32},{64,48},{80,64},{96,80},{112,96},{17,1},{33... | collective-permute-start | bytes 3145736 | tf_op jit(solution)/shard_map/while/body/eval_jaxpr/ppermute | solution.py:15
  543.3 43.2 %copy-start.1 = (bf16[128,256]{1,0:T(8,128)(2,1)S(1)}, bf16[128,256]{1,0:T(8,128)(2,1)}, u32[]{:S(2)}) copy-start(bf16[128,256]{1,0:T(8,128)(2,1)} %add_convert_fusion.4) | copy-start | bytes 196612 | tf_op jit(solution)/shard_map/while
  543.3 103.9 %all-gather.5.cloned.1.call-start = ((), (), s32[]{:S(2)}) async-start(), calls=%async_computation.2 | async-start | bytes 1114112 | tf_op jit(solution)/shard_map/while/body/eval_jaxpr/all_gather | solution.py:77
  647.3 73.8 %all-gather.3.cloned.1.call-start = ((), (), s32[]{:S(2)}) async-start(), calls=%async_computation.1 | async-start | bytes 1114112 | tf_op jit(solution)/shard_map/while/body/eval_jaxpr/all_gather | solution.py:73
  647.3 31.4 %collective-permute-start = (bf16[128,4096]{1,0:T(8,128)(2,1)}, bf16[128,4096]{1,0:T(8,128)(2,1)S(1)}, u32[]{:S(2)}, u32[]{:S(2)}) collective-permute-start(bf16[128,4096]{1,0:T(8,128)(2,1)} %get-tuple-element.465), channel_id=1, source_target_pairs={{16,0},{32,16},{48,32},{64,48},{80,64},{96,80},{112,96},{17,1},{33... | collective-permute-start | bytes 3145736 | tf_op jit(solution)/shard_map/while/body/eval_jaxpr/ppermute | solution.py:15
  683.3 43.2 %copy-start.1 = (bf16[128,256]{1,0:T(8,128)(2,1)S(1)}, bf16[128,256]{1,0:T(8,128)(2,1)}, u32[]{:S(2)}) copy-start(bf16[128,256]{1,0:T(8,128)(2,1)} %add_convert_fusion.4) | copy-start | bytes 196612 | tf_op jit(solution)/shard_map/while
  683.3 103.9 %all-gather.5.cloned.1.call-start = ((), (), s32[]{:S(2)}) async-start(), calls=%async_computation.2 | async-start | bytes 1114112 | tf_op jit(solution)/shard_map/while/body/eval_jaxpr/all_gather | solution.py:77
  787.3 73.8 %all-gather.3.cloned.1.call-start = ((), (), s32[]{:S(2)}) async-start(), calls=%async_computation.1 | async-start | bytes 1114112 | tf_op jit(solution)/shard_map/while/body/eval_jaxpr/all_gather | solution.py:73
  787.3 31.4 %collective-permute-start = (bf16[128,4096]{1,0:T(8,128)(2,1)}, bf16[128,4096]{1,0:T(8,128)(2,1)S(1)}, u32[]{:S(2)}, u32[]{:S(2)}) collective-permute-start(bf16[128,4096]{1,0:T(8,128)(2,1)} %get-tuple-element.465), channel_id=1, source_target_pairs={{16,0},{32,16},{48,32},{64,48},{80,64},{96,80},{112,96},{17,1},{33... | collective-permute-start | bytes 3145736 | tf_op jit(solution)/shard_map/while/body/eval_jaxpr/ppermute | solution.py:15
  823.3 43.2 %copy-start.1 = (bf16[128,256]{1,0:T(8,128)(2,1)S(1)}, bf16[128,256]{1,0:T(8,128)(2,1)}, u32[]{:S(2)}) copy-start(bf16[128,256]{1,0:T(8,128)(2,1)} %add_convert_fusion.4) | copy-start | bytes 196612 | tf_op jit(solution)/shard_map/while
  823.4 103.9 %all-gather.5.cloned.1.call-start = ((), (), s32[]{:S(2)}) async-start(), calls=%async_computation.2 | async-start | bytes 1114112 | tf_op jit(solution)/shard_map/while/body/eval_jaxpr/all_gather | solution.py:77
  927.3 73.8 %all-gather.3.cloned.1.call-start = ((), (), s32[]{:S(2)}) async-start(), calls=%async_computation.1 | async-start | bytes 1114112 | tf_op jit(solution)/shard_map/while/body/eval_jaxpr/all_gather | solution.py:73
  927.4 31.4 %collective-permute-start = (bf16[128,4096]{1,0:T(8,128)(2,1)}, bf16[128,4096]{1,0:T(8,128)(2,1)S(1)}, u32[]{:S(2)}, u32[]{:S(2)}) collective-permute-start(bf16[128,4096]{1,0:T(8,128)(2,1)} %get-tuple-element.465), channel_id=1, source_target_pairs={{16,0},{32,16},{48,32},{64,48},{80,64},{96,80},{112,96},{17,1},{33... | collective-permute-start | bytes 3145736 | tf_op jit(solution)/shard_map/while/body/eval_jaxpr/ppermute | solution.py:15
  963.4 43.2 %copy-start.1 = (bf16[128,256]{1,0:T(8,128)(2,1)S(1)}, bf16[128,256]{1,0:T(8,128)(2,1)}, u32[]{:S(2)}) copy-start(bf16[128,256]{1,0:T(8,128)(2,1)} %add_convert_fusion.4) | copy-start | bytes 196612 | tf_op jit(solution)/shard_map/while
  963.4 103.9 %all-gather.5.cloned.1.call-start = ((), (), s32[]{:S(2)}) async-start(), calls=%async_computation.2 | async-start | bytes 1114112 | tf_op jit(solution)/shard_map/while/body/eval_jaxpr/all_gather | solution.py:77
  1067.3 73.8 %all-gather.3.cloned.1.call-start = ((), (), s32[]{:S(2)}) async-start(), calls=%async_computation.1 | async-start | bytes 1114112 | tf_op jit(solution)/shard_map/while/body/eval_jaxpr/all_gather | solution.py:73
  1067.4 31.4 %collective-permute-start = (bf16[128,4096]{1,0:T(8,128)(2,1)}, bf16[128,4096]{1,0:T(8,128)(2,1)S(1)}, u32[]{:S(2)}, u32[]{:S(2)}) collective-permute-start(bf16[128,4096]{1,0:T(8,128)(2,1)} %get-tuple-element.465), channel_id=1, source_target_pairs={{16,0},{32,16},{48,32},{64,48},{80,64},{96,80},{112,96},{17,1},{33... | collective-permute-start | bytes 3145736 | tf_op jit(solution)/shard_map/while/body/eval_jaxpr/ppermute | solution.py:15
  1103.4 43.2 %copy-start.1 = (bf16[128,256]{1,0:T(8,128)(2,1)S(1)}, bf16[128,256]{1,0:T(8,128)(2,1)}, u32[]{:S(2)}) copy-start(bf16[128,256]{1,0:T(8,128)(2,1)} %add_convert_fusion.4) | copy-start | bytes 196612 | tf_op jit(solution)/shard_map/while
  1103.4 103.9 %all-gather.5.cloned.1.call-start = ((), (), s32[]{:S(2)}) async-start(), calls=%async_computation.2 | async-start | bytes 1114112 | tf_op jit(solution)/shard_map/while/body/eval_jaxpr/all_gather | solution.py:77
  1207.4 73.8 %all-gather.3.cloned.1.call-start = ((), (), s32[]{:S(2)}) async-start(), calls=%async_computation.1 | async-start | bytes 1114112 | tf_op jit(solution)/shard_map/while/body/eval_jaxpr/all_gather | solution.py:73
  1207.4 31.4 %collective-permute-start = (bf16[128,4096]{1,0:T(8,128)(2,1)}, bf16[128,4096]{1,0:T(8,128)(2,1)S(1)}, u32[]{:S(2)}, u32[]{:S(2)}) collective-permute-start(bf16[128,4096]{1,0:T(8,128)(2,1)} %get-tuple-element.465), channel_id=1, source_target_pairs={{16,0},{32,16},{48,32},{64,48},{80,64},{96,80},{112,96},{17,1},{33... | collective-permute-start | bytes 3145736 | tf_op jit(solution)/shard_map/while/body/eval_jaxpr/ppermute | solution.py:15
  1243.4 43.2 %copy-start.1 = (bf16[128,256]{1,0:T(8,128)(2,1)S(1)}, bf16[128,256]{1,0:T(8,128)(2,1)}, u32[]{:S(2)}) copy-start(bf16[128,256]{1,0:T(8,128)(2,1)} %add_convert_fusion.4) | copy-start | bytes 196612 | tf_op jit(solution)/shard_map/while
  1243.4 103.9 %all-gather.5.cloned.1.call-start = ((), (), s32[]{:S(2)}) async-start(), calls=%async_computation.2 | async-start | bytes 1114112 | tf_op jit(solution)/shard_map/while/body/eval_jaxpr/all_gather | solution.py:77
  1347.4 73.8 %all-gather.3.cloned.1.call-start = ((), (), s32[]{:S(2)}) async-start(), calls=%async_computation.1 | async-start | bytes 1114112 | tf_op jit(solution)/shard_map/while/body/eval_jaxpr/all_gather | solution.py:73
  1347.4 31.4 %collective-permute-start = (bf16[128,4096]{1,0:T(8,128)(2,1)}, bf16[128,4096]{1,0:T(8,128)(2,1)S(1)}, u32[]{:S(2)}, u32[]{:S(2)}) collective-permute-start(bf16[128,4096]{1,0:T(8,128)(2,1)} %get-tuple-element.465), channel_id=1, source_target_pairs={{16,0},{32,16},{48,32},{64,48},{80,64},{96,80},{112,96},{17,1},{33... | collective-permute-start | bytes 3145736 | tf_op jit(solution)/shard_map/while/body/eval_jaxpr/ppermute | solution.py:15
  1383.4 43.2 %copy-start.1 = (bf16[128,256]{1,0:T(8,128)(2,1)S(1)}, bf16[128,256]{1,0:T(8,128)(2,1)}, u32[]{:S(2)}) copy-start(bf16[128,256]{1,0:T(8,128)(2,1)} %add_convert_fusion.4) | copy-start | bytes 196612 | tf_op jit(solution)/shard_map/while
  1383.5 103.9 %all-gather.5.cloned.1.call-start = ((), (), s32[]{:S(2)}) async-start(), calls=%async_computation.2 | async-start | bytes 1114112 | tf_op jit(solution)/shard_map/while/body/eval_jaxpr/all_gather | solution.py:77
  1487.4 73.8 %all-gather.3.cloned.1.call-start = ((), (), s32[]{:S(2)}) async-start(), calls=%async_computation.1 | async-start | bytes 1114112 | tf_op jit(solution)/shard_map/while/body/eval_jaxpr/all_gather | solution.py:73
  1487.5 31.4 %collective-permute-start = (bf16[128,4096]{1,0:T(8,128)(2,1)}, bf16[128,4096]{1,0:T(8,128)(2,1)S(1)}, u32[]{:S(2)}, u32[]{:S(2)}) collective-permute-start(bf16[128,4096]{1,0:T(8,128)(2,1)} %get-tuple-element.465), channel_id=1, source_target_pairs={{16,0},{32,16},{48,32},{64,48},{80,64},{96,80},{112,96},{17,1},{33... | collective-permute-start | bytes 3145736 | tf_op jit(solution)/shard_map/while/body/eval_jaxpr/ppermute | solution.py:15
  1523.5 43.2 %copy-start.1 = (bf16[128,256]{1,0:T(8,128)(2,1)S(1)}, bf16[128,256]{1,0:T(8,128)(2,1)}, u32[]{:S(2)}) copy-start(bf16[128,256]{1,0:T(8,128)(2,1)} %add_convert_fusion.4) | copy-start | bytes 196612 | tf_op jit(solution)/shard_map/while
  1523.5 103.9 %all-gather.5.cloned.1.call-start = ((), (), s32[]{:S(2)}) async-start(), calls=%async_computation.2 | async-start | bytes 1114112 | tf_op jit(solution)/shard_map/while/body/eval_jaxpr/all_gather | solution.py:77
  (1 other events, 2.3 us)
Sparse Core Ops, SparseCore 0:
  10.5 86.3 all-reduce.1
  120.3 40.5 all-gather.2
  164.4 42.9 all-gather.4
  263.4 37.5 all-gather.2
  304.4 42.9 all-gather.4
  403.4 37.5 all-gather.2
  444.4 42.9 all-gather.4
  543.4 37.5 all-gather.2
  584.5 42.9 all-gather.4
  683.4 37.5 all-gather.2
  724.5 42.9 all-gather.4
  823.5 37.5 all-gather.2
  864.5 42.9 all-gather.4
  963.5 37.5 all-gather.2
  1004.5 42.9 all-gather.4
  1103.5 37.5 all-gather.2
  1144.6 42.9 all-gather.4
  1243.5 37.5 all-gather.2
  1284.6 42.9 all-gather.4
  1383.6 37.5 all-gather.2
  1424.6 42.9 all-gather.4
  1523.6 37.5 all-gather.2
  1564.6 42.9 all-gather.4
where the time goes:
time: 1660 us
  blocking collectives  671 us (40%)
  waiting for transfers between devices  657 us (40%)
  starting transfers between devices  182 us (11%)
  matrix products  95 us (6%)
  other arithmetic  26.3 us (2%)
  local copies, waits for them, and re-layouts  17.8 us (1%)
    psum x11, blocking collectives, tick(): lax.psum(partial_out.reshape(block_rows, -1), 'tp')  643 us
    all_gather x11, waiting for transfers between devices, tick(): lax.all_gather(middle_own, 'tp', axis=1, tiled=True)  417 us
    ppermute x11, starting transfers between devices, from_behind(): return lax.ppermute(value, axis, pairs)  181 us
    ppermute x11, waiting for transfers between devices, from_behind(): return lax.ppermute(value, axis, pairs)  151 us
    psum x1, waiting for transfers between devices, shards(): lax.psum(partial_in.reshape(total_tokens, -1), 'tp')  87.7 us
    dot_general x11, matrix products, contract_columns(): lax.dot_general(portion, matrix, (((1,), (1,)), ((), ())), preferred_elem...  36.4 us
    dot_general x11, matrix products, tick(): lax.dot_general(upper_full, weights[1], (((1,), (1,)), ((), ())), preferr...  33.7 us
  transfers between devices with their start and end apart: 34, of which 23 were waited for; matrix products, arithmetic and copies ran while one was open for 3% of the time, Pallas kernels for 0%

commit v1 on v0

--- a/solution.py
+++ b/solution.py
@@ -79,7 +79,9 @@
         partial_out = jnp.einsum(
             "lrd,ldk->rlk", cotangents, output_basis, preferred_element_type=jnp.float32
         )
-        out_feats = lax.psum(partial_out.reshape(block_rows, -1), "tp").reshape(partial_out.shape)
+        out_feats = jnp.sum(
+            lax.all_gather(partial_out.reshape(block_rows, -1), "tp"), axis=0
+        ).reshape(partial_out.shape)
         in_block = lax.dynamic_slice_in_dim(in_feats, first_row, block_rows, 0)
         block_examples = jnp.repeat(
             lax.dynamic_slice_in_dim(sequence_example, micro_clip * SEQ_MB, SEQ_MB, 0), SEQLEN

time: 1660 us -> 1330 us (0.80)
  blocking collectives: 671 us -> 223 us
  waiting for transfers between devices: 657 us -> 903 us
  starting transfers between devices: 182 us -> 43.7 us
    psum x11 -> x0, blocking collectives: 643 us -> none  [tick(): lax.psum(partial_out.reshape(block_rows, -1), 'tp')]
    all_gather x11, waiting for transfers between devices: 0.19 us -> 217 us  [tick(): new_outgoing = lax.all_gather(lower_own, 'tp', axis=1, tiled=True)]
    all_gather x0 -> x11, blocking collectives: none -> 208 us  [tick(): lax.all_gather(partial_out.reshape(block_rows, -1), 'tp')]
    ppermute x11, starting transfers between devices: 181 us -> 43.2 us  [from_behind(): return lax.ppermute(value, axis, pairs)]
    all_gather x11, waiting for transfers between devices: 417 us -> 447 us  [tick(): lax.all_gather(middle_own, 'tp', axis=1, tiled=True)]
  transfers between devices with their start and end apart: 34 -> 34, of which waited for: 23 -> 34; matrix products, arithmetic and copies ran while one was open for 3% -> 4% of each run, Pallas kernels for 0% -> 0%
where the time goes in v1:
time: 1330 us; the launch traced here: 1320 us
  waiting for transfers between devices  903 us (68%)
  blocking collectives  223 us (17%)
  matrix products  95 us (7%)
  starting transfers between devices  43.7 us (3%)
  other arithmetic  26.7 us (2%)
  local copies, waits for them, and re-layouts  17.8 us (1%)
    all_gather x11, waiting for transfers between devices, tick(): lax.all_gather(middle_own, 'tp', axis=1, tiled=True)  447 us
    all_gather x11, waiting for transfers between devices, tick(): new_outgoing = lax.all_gather(lower_own, 'tp', axis=1, tiled=True)  217 us
    all_gather x11, blocking collectives, tick(): lax.all_gather(partial_out.reshape(block_rows, -1), 'tp')  208 us
    ppermute x11, waiting for transfers between devices, from_behind(): return lax.ppermute(value, axis, pairs)  151 us
    psum x1, waiting for transfers between devices, shards(): lax.psum(partial_in.reshape(total_tokens, -1), 'tp')  87.7 us
    ppermute x11, starting transfers between devices, from_behind(): return lax.ppermute(value, axis, pairs)  43.2 us
    dot_general x11, matrix products, contract_columns(): lax.dot_general(portion, matrix, (((1,), (1,)), ((), ())), preferred_elem...  36.4 us
    dot_general x11, matrix products, tick(): lax.dot_general(upper_full, weights[1], (((1,), (1,)), ((), ())), preferr...  33.6 us
  transfers between devices with their start and end apart: 34, of which 34 were waited for; matrix products, arithmetic and copies ran while one was open for 4% of the time, Pallas kernels for 0%

profile of v1, /device:TPU:1, one launch (start us, length us, event | category | flops | bytes accessed | tf_op | source)
XLA Modules:
  0.0 1323.0 jit_solution(3568479040223697870)
XLA Ops:
  9.2 87.7 %all-reduce.2.cloned.1.call-done = f32[512,2,64]{0,2,1:T(8,128)} async-done(((f32[512,2,64]{0,2,1:T(8,128)}), f32[512,2,64]{0,2,1:T(8,128)}) %all-reduce.2.cloned.1.call-update) | async-done | bytes 262160 | tf_op jit(solution)/shard_map/psum | solution.py:49
  98.0 1203.8 %while.18 = (s32[]{:T(128)}, bf16[128,4096]{1,0:T(8,128)(2,1)}, f32[2,2,2048]{2,1,0:T(2,128)S(1)}, pred[]{:T(512)}, s32[]{:T(128)}, /*index=5*/bf16[512,4096]{1,...) while((s32[]{:T(128)}, bf16[128,4096]{1,0:T(8,128)(2,1)}, ...), condition=%wide.region_3.4_spmd.clone, body=%wide.region_1.3_spmd.clone.sunk | while | flops 555163648 | bytes 27034632 | solution.py:103
  101.9 13.7 %collective-permute-done = bf16[128,4096]{1,0:T(8,128)(2,1)S(1)} collective-permute-done((bf16[128,4096]{1,0:T(8,128)(2,1)}, bf16[128,4096]{1,0:T(8,128)(2,1)S(1)}, u32[]{:S(2)}, u32[]{:S(2)}) %collective-permute-start) | collective-permute-done | bytes 1048608 | tf_op jit(solution)/shard_map/while/body/eval_jaxpr/ppermute | solution.py:15
  120.3 40.6 %all-gather.3.cloned.1.call-done = bf16[128,4096]{1,0:T(8,128)(2,1)} async-done(((bf16[128,256]{1,0:T(8,128)(2,1)}), bf16[128,4096]{1,0:T(8,128)(2,1)}) %all-gather.3.cloned.1.call-update) | async-done | bytes 1048592 | tf_op jit(solution)/shard_map/while/body/eval_jaxpr/all_gather | solution.py:73
  166.6 18.9 %all_gather.35 = f32[16,128,64]{1,2,0:T(8,128)S(1)} all-gather(f32[1,128,64]{1,2,0:T(8,128)S(1)} %bitcast.83), channel_id=1, replica_groups=mesh['section'=8,'tp'=16] {'tp'}, dimensions={0}, use_global_device_ids=true | all-gather | bytes 557056 | tf_op jit(solution)/shard_map/while/body/eval_jaxpr/all_gather | solution.py:83
  187.7 19.7 %all-gather.5.cloned.1.call-done = bf16[128,4096]{1,0:T(8,128)(2,1)} async-done(((bf16[128,256]{1,0:T(8,128)(2,1)}), bf16[128,4096]{1,0:T(8,128)(2,1)}) %all-gather.5.cloned.1.call-update) | async-done | bytes 1048592 | tf_op jit(solution)/shard_map/while/body/eval_jaxpr/all_gather | solution.py:77
  207.4 3.9 collective-permute-start
  211.4 13.7 %collective-permute-done = bf16[128,4096]{1,0:T(8,128)(2,1)S(1)} collective-permute-done((bf16[128,4096]{1,0:T(8,128)(2,1)}, bf16[128,4096]{1,0:T(8,128)(2,1)S(1)}, u32[]{:S(2)}, u32[]{:S(2)}) %collective-permute-start) | collective-permute-done | bytes 1048608 | tf_op jit(solution)/shard_map/while/body/eval_jaxpr/ppermute | solution.py:15
  229.7 40.6 %all-gather.3.cloned.1.call-done = bf16[128,4096]{1,0:T(8,128)(2,1)} async-done(((bf16[128,256]{1,0:T(8,128)(2,1)}), bf16[128,4096]{1,0:T(8,128)(2,1)}) %all-gather.3.cloned.1.call-update) | async-done | bytes 1048592 | tf_op jit(solution)/shard_map/while/body/eval_jaxpr/all_gather | solution.py:73
  276.0 18.9 %all_gather.35 = f32[16,128,64]{1,2,0:T(8,128)S(1)} all-gather(f32[1,128,64]{1,2,0:T(8,128)S(1)} %bitcast.83), channel_id=1, replica_groups=mesh['section'=8,'tp'=16] {'tp'}, dimensions={0}, use_global_device_ids=true | all-gather | bytes 557056 | tf_op jit(solution)/shard_map/while/body/eval_jaxpr/all_gather | solution.py:83
  297.1 19.7 %all-gather.5.cloned.1.call-done = bf16[128,4096]{1,0:T(8,128)(2,1)} async-done(((bf16[128,256]{1,0:T(8,128)(2,1)}), bf16[128,4096]{1,0:T(8,128)(2,1)}) %all-gather.5.cloned.1.call-update) | async-done | bytes 1048592 | tf_op jit(solution)/shard_map/while/body/eval_jaxpr/all_gather | solution.py:77
  320.8 13.7 %collective-permute-done = bf16[128,4096]{1,0:T(8,128)(2,1)S(1)} collective-permute-done((bf16[128,4096]{1,0:T(8,128)(2,1)}, bf16[128,4096]{1,0:T(8,128)(2,1)S(1)}, u32[]{:S(2)}, u32[]{:S(2)}) %collective-permute-start) | collective-permute-done | bytes 1048608 | tf_op jit(solution)/shard_map/while/body/eval_jaxpr/ppermute | solution.py:15
  339.1 40.6 %all-gather.3.cloned.1.call-done = bf16[128,4096]{1,0:T(8,128)(2,1)} async-done(((bf16[128,256]{1,0:T(8,128)(2,1)}), bf16[128,4096]{1,0:T(8,128)(2,1)}) %all-gather.3.cloned.1.call-update) | async-done | bytes 1048592 | tf_op jit(solution)/shard_map/while/body/eval_jaxpr/all_gather | solution.py:73
  385.5 18.9 %all_gather.35 = f32[16,128,64]{1,2,0:T(8,128)S(1)} all-gather(f32[1,128,64]{1,2,0:T(8,128)S(1)} %bitcast.83), channel_id=1, replica_groups=mesh['section'=8,'tp'=16] {'tp'}, dimensions={0}, use_global_device_ids=true | all-gather | bytes 557056 | tf_op jit(solution)/shard_map/while/body/eval_jaxpr/all_gather | solution.py:83
  406.6 19.7 %all-gather.5.cloned.1.call-done = bf16[128,4096]{1,0:T(8,128)(2,1)} async-done(((bf16[128,256]{1,0:T(8,128)(2,1)}), bf16[128,4096]{1,0:T(8,128)(2,1)}) %all-gather.5.cloned.1.call-update) | async-done | bytes 1048592 | tf_op jit(solution)/shard_map/while/body/eval_jaxpr/all_gather | solution.py:77
  430.2 13.7 %collective-permute-done = bf16[128,4096]{1,0:T(8,128)(2,1)S(1)} collective-permute-done((bf16[128,4096]{1,0:T(8,128)(2,1)}, bf16[128,4096]{1,0:T(8,128)(2,1)S(1)}, u32[]{:S(2)}, u32[]{:S(2)}) %collective-permute-start) | collective-permute-done | bytes 1048608 | tf_op jit(solution)/shard_map/while/body/eval_jaxpr/ppermute | solution.py:15
  448.6 40.6 %all-gather.3.cloned.1.call-done = bf16[128,4096]{1,0:T(8,128)(2,1)} async-done(((bf16[128,256]{1,0:T(8,128)(2,1)}), bf16[128,4096]{1,0:T(8,128)(2,1)}) %all-gather.3.cloned.1.call-update) | async-done | bytes 1048592 | tf_op jit(solution)/shard_map/while/body/eval_jaxpr/all_gather | solution.py:73
  494.9 18.9 %all_gather.35 = f32[16,128,64]{1,2,0:T(8,128)S(1)} all-gather(f32[1,128,64]{1,2,0:T(8,128)S(1)} %bitcast.83), channel_id=1, replica_groups=mesh['section'=8,'tp'=16] {'tp'}, dimensions={0}, use_global_device_ids=true | all-gather | bytes 557056 | tf_op jit(solution)/shard_map/while/body/eval_jaxpr/all_gather | solution.py:83
  516.0 19.7 %all-gather.5.cloned.1.call-done = bf16[128,4096]{1,0:T(8,128)(2,1)} async-done(((bf16[128,256]{1,0:T(8,128)(2,1)}), bf16[128,4096]{1,0:T(8,128)(2,1)}) %all-gather.5.cloned.1.call-update) | async-done | bytes 1048592 | tf_op jit(solution)/shard_map/while/body/eval_jaxpr/all_gather | solution.py:77
  539.7 13.7 %collective-permute-done = bf16[128,4096]{1,0:T(8,128)(2,1)S(1)} collective-permute-done((bf16[128,4096]{1,0:T(8,128)(2,1)}, bf16[128,4096]{1,0:T(8,128)(2,1)S(1)}, u32[]{:S(2)}, u32[]{:S(2)}) %collective-permute-start) | collective-permute-done | bytes 1048608 | tf_op jit(solution)/shard_map/while/body/eval_jaxpr/ppermute | solution.py:15
  558.0 40.6 %all-gather.3.cloned.1.call-done = bf16[128,4096]{1,0:T(8,128)(2,1)} async-done(((bf16[128,256]{1,0:T(8,128)(2,1)}), bf16[128,4096]{1,0:T(8,128)(2,1)}) %all-gather.3.cloned.1.call-update) | async-done | bytes 1048592 | tf_op jit(solution)/shard_map/while/body/eval_jaxpr/all_gather | solution.py:73
  604.3 18.9 %all_gather.35 = f32[16,128,64]{1,2,0:T(8,128)S(1)} all-gather(f32[1,128,64]{1,2,0:T(8,128)S(1)} %bitcast.83), channel_id=1, replica_groups=mesh['section'=8,'tp'=16] {'tp'}, dimensions={0}, use_global_device_ids=true | all-gather | bytes 557056 | tf_op jit(solution)/shard_map/while/body/eval_jaxpr/all_gather | solution.py:83
  625.5 19.7 %all-gather.5.cloned.1.call-done = bf16[128,4096]{1,0:T(8,128)(2,1)} async-done(((bf16[128,256]{1,0:T(8,128)(2,1)}), bf16[128,4096]{1,0:T(8,128)(2,1)}) %all-gather.5.cloned.1.call-update) | async-done | bytes 1048592 | tf_op jit(solution)/shard_map/while/body/eval_jaxpr/all_gather | solution.py:77
  649.1 13.7 %collective-permute-done = bf16[128,4096]{1,0:T(8,128)(2,1)S(1)} collective-permute-done((bf16[128,4096]{1,0:T(8,128)(2,1)}, bf16[128,4096]{1,0:T(8,128)(2,1)S(1)}, u32[]{:S(2)}, u32[]{:S(2)}) %collective-permute-start) | collective-permute-done | bytes 1048608 | tf_op jit(solution)/shard_map/while/body/eval_jaxpr/ppermute | solution.py:15
  667.5 40.6 %all-gather.3.cloned.1.call-done = bf16[128,4096]{1,0:T(8,128)(2,1)} async-done(((bf16[128,256]{1,0:T(8,128)(2,1)}), bf16[128,4096]{1,0:T(8,128)(2,1)}) %all-gather.3.cloned.1.call-update) | async-done | bytes 1048592 | tf_op jit(solution)/shard_map/while/body/eval_jaxpr/all_gather | solution.py:73
  713.8 18.9 %all_gather.35 = f32[16,128,64]{1,2,0:T(8,128)S(1)} all-gather(f32[1,128,64]{1,2,0:T(8,128)S(1)} %bitcast.83), channel_id=1, replica_groups=mesh['section'=8,'tp'=16] {'tp'}, dimensions={0}, use_global_device_ids=true | all-gather | bytes 557056 | tf_op jit(solution)/shard_map/while/body/eval_jaxpr/all_gather | solution.py:83
  734.9 19.7 %all-gather.5.cloned.1.call-done = bf16[128,4096]{1,0:T(8,128)(2,1)} async-done(((bf16[128,256]{1,0:T(8,128)(2,1)}), bf16[128,4096]{1,0:T(8,128)(2,1)}) %all-gather.5.cloned.1.call-update) | async-done | bytes 1048592 | tf_op jit(solution)/shard_map/while/body/eval_jaxpr/all_gather | solution.py:77
  758.6 13.7 %collective-permute-done = bf16[128,4096]{1,0:T(8,128)(2,1)S(1)} collective-permute-done((bf16[128,4096]{1,0:T(8,128)(2,1)}, bf16[128,4096]{1,0:T(8,128)(2,1)S(1)}, u32[]{:S(2)}, u32[]{:S(2)}) %collective-permute-start) | collective-permute-done | bytes 1048608 | tf_op jit(solution)/shard_map/while/body/eval_jaxpr/ppermute | solution.py:15
  776.9 40.6 %all-gather.3.cloned.1.call-done = bf16[128,4096]{1,0:T(8,128)(2,1)} async-done(((bf16[128,256]{1,0:T(8,128)(2,1)}), bf16[128,4096]{1,0:T(8,128)(2,1)}) %all-gather.3.cloned.1.call-update) | async-done | bytes 1048592 | tf_op jit(solution)/shard_map/while/body/eval_jaxpr/all_gather | solution.py:73
  823.2 18.9 %all_gather.35 = f32[16,128,64]{1,2,0:T(8,128)S(1)} all-gather(f32[1,128,64]{1,2,0:T(8,128)S(1)} %bitcast.83), channel_id=1, replica_groups=mesh['section'=8,'tp'=16] {'tp'}, dimensions={0}, use_global_device_ids=true | all-gather | bytes 557056 | tf_op jit(solution)/shard_map/while/body/eval_jaxpr/all_gather | solution.py:83
  844.3 19.7 %all-gather.5.cloned.1.call-done = bf16[128,4096]{1,0:T(8,128)(2,1)} async-done(((bf16[128,256]{1,0:T(8,128)(2,1)}), bf16[128,4096]{1,0:T(8,128)(2,1)}) %all-gather.5.cloned.1.call-update) | async-done | bytes 1048592 | tf_op jit(solution)/shard_map/while/body/eval_jaxpr/all_gather | solution.py:77
  868.0 13.7 %collective-permute-done = bf16[128,4096]{1,0:T(8,128)(2,1)S(1)} collective-permute-done((bf16[128,4096]{1,0:T(8,128)(2,1)}, bf16[128,4096]{1,0:T(8,128)(2,1)S(1)}, u32[]{:S(2)}, u32[]{:S(2)}) %collective-permute-start) | collective-permute-done | bytes 1048608 | tf_op jit(solution)/shard_map/while/body/eval_jaxpr/ppermute | solution.py:15
  886.3 40.6 %all-gather.3.cloned.1.call-done = bf16[128,4096]{1,0:T(8,128)(2,1)} async-done(((bf16[128,256]{1,0:T(8,128)(2,1)}), bf16[128,4096]{1,0:T(8,128)(2,1)}) %all-gather.3.cloned.1.call-update) | async-done | bytes 1048592 | tf_op jit(solution)/shard_map/while/body/eval_jaxpr/all_gather | solution.py:73
  932.7 18.9 %all_gather.35 = f32[16,128,64]{1,2,0:T(8,128)S(1)} all-gather(f32[1,128,64]{1,2,0:T(8,128)S(1)} %bitcast.83), channel_id=1, replica_groups=mesh['section'=8,'tp'=16] {'tp'}, dimensions={0}, use_global_device_ids=true | all-gather | bytes 557056 | tf_op jit(solution)/shard_map/while/body/eval_jaxpr/all_gather | solution.py:83
  953.8 19.7 %all-gather.5.cloned.1.call-done = bf16[128,4096]{1,0:T(8,128)(2,1)} async-done(((bf16[128,256]{1,0:T(8,128)(2,1)}), bf16[128,4096]{1,0:T(8,128)(2,1)}) %all-gather.5.cloned.1.call-update) | async-done | bytes 1048592 | tf_op jit(solution)/shard_map/while/body/eval_jaxpr/all_gather | solution.py:77
  977.4 13.7 %collective-permute-done = bf16[128,4096]{1,0:T(8,128)(2,1)S(1)} collective-permute-done((bf16[128,4096]{1,0:T(8,128)(2,1)}, bf16[128,4096]{1,0:T(8,128)(2,1)S(1)}, u32[]{:S(2)}, u32[]{:S(2)}) %collective-permute-start) | collective-permute-done | bytes 1048608 | tf_op jit(solution)/shard_map/while/body/eval_jaxpr/ppermute | solution.py:15
  995.8 40.6 %all-gather.3.cloned.1.call-done = bf16[128,4096]{1,0:T(8,128)(2,1)} async-done(((bf16[128,256]{1,0:T(8,128)(2,1)}), bf16[128,4096]{1,0:T(8,128)(2,1)}) %all-gather.3.cloned.1.call-update) | async-done | bytes 1048592 | tf_op jit(solution)/shard_map/while/body/eval_jaxpr/all_gather | solution.py:73
  1042.1 18.9 %all_gather.35 = f32[16,128,64]{1,2,0:T(8,128)S(1)} all-gather(f32[1,128,64]{1,2,0:T(8,128)S(1)} %bitcast.83), channel_id=1, replica_groups=mesh['section'=8,'tp'=16] {'tp'}, dimensions={0}, use_global_device_ids=true | all-gather | bytes 557056 | tf_op jit(solution)/shard_map/while/body/eval_jaxpr/all_gather | solution.py:83
  1063.2 19.7 %all-gather.5.cloned.1.call-done = bf16[128,4096]{1,0:T(8,128)(2,1)} async-done(((bf16[128,256]{1,0:T(8,128)(2,1)}), bf16[128,4096]{1,0:T(8,128)(2,1)}) %all-gather.5.cloned.1.call-update) | async-done | bytes 1048592 | tf_op jit(solution)/shard_map/while/body/eval_jaxpr/all_gather | solution.py:77
  1086.9 13.7 %collective-permute-done = bf16[128,4096]{1,0:T(8,128)(2,1)S(1)} collective-permute-done((bf16[128,4096]{1,0:T(8,128)(2,1)}, bf16[128,4096]{1,0:T(8,128)(2,1)S(1)}, u32[]{:S(2)}, u32[]{:S(2)}) %collective-permute-start) | collective-permute-done | bytes 1048608 | tf_op jit(solution)/shard_map/while/body/eval_jaxpr/ppermute | solution.py:15
  1105.2 40.6 %all-gather.3.cloned.1.call-done = bf16[128,4096]{1,0:T(8,128)(2,1)} async-done(((bf16[128,256]{1,0:T(8,128)(2,1)}), bf16[128,4096]{1,0:T(8,128)(2,1)}) %all-gather.3.cloned.1.call-update) | async-done | bytes 1048592 | tf_op jit(solution)/shard_map/while/body/eval_jaxpr/all_gather | solution.py:73
  1151.5 18.9 %all_gather.35 = f32[16,128,64]{1,2,0:T(8,128)S(1)} all-gather(f32[1,128,64]{1,2,0:T(8,128)S(1)} %bitcast.83), channel_id=1, replica_groups=mesh['section'=8,'tp'=16] {'tp'}, dimensions={0}, use_global_device_ids=true | all-gather | bytes 557056 | tf_op jit(solution)/shard_map/while/body/eval_jaxpr/all_gather | solution.py:83
  1172.7 19.7 %all-gather.5.cloned.1.call-done = bf16[128,4096]{1,0:T(8,128)(2,1)} async-done(((bf16[128,256]{1,0:T(8,128)(2,1)}), bf16[128,4096]{1,0:T(8,128)(2,1)}) %all-gather.5.cloned.1.call-update) | async-done | bytes 1048592 | tf_op jit(solution)/shard_map/while/body/eval_jaxpr/all_gather | solution.py:77
  1196.3 13.7 %collective-permute-done = bf16[128,4096]{1,0:T(8,128)(2,1)S(1)} collective-permute-done((bf16[128,4096]{1,0:T(8,128)(2,1)}, bf16[128,4096]{1,0:T(8,128)(2,1)S(1)}, u32[]{:S(2)}, u32[]{:S(2)}) %collective-permute-start) | collective-permute-done | bytes 1048608 | tf_op jit(solution)/shard_map/while/body/eval_jaxpr/ppermute | solution.py:15
  1214.7 40.6 %all-gather.3.cloned.1.call-done = bf16[128,4096]{1,0:T(8,128)(2,1)} async-done(((bf16[128,256]{1,0:T(8,128)(2,1)}), bf16[128,4096]{1,0:T(8,128)(2,1)}) %all-gather.3.cloned.1.call-update) | async-done | bytes 1048592 | tf_op jit(solution)/shard_map/while/body/eval_jaxpr/all_gather | solution.py:73
  1261.0 18.9 %all_gather.35 = f32[16,128,64]{1,2,0:T(8,128)S(1)} all-gather(f32[1,128,64]{1,2,0:T(8,128)S(1)} %bitcast.83), channel_id=1, replica_groups=mesh['section'=8,'tp'=16] {'tp'}, dimensions={0}, use_global_device_ids=true | all-gather | bytes 557056 | tf_op jit(solution)/shard_map/while/body/eval_jaxpr/all_gather | solution.py:83
  1282.1 19.7 %all-gather.5.cloned.1.call-done = bf16[128,4096]{1,0:T(8,128)(2,1)} async-done(((bf16[128,256]{1,0:T(8,128)(2,1)}), bf16[128,4096]{1,0:T(8,128)(2,1)}) %all-gather.5.cloned.1.call-update) | async-done | bytes 1048592 | tf_op jit(solution)/shard_map/while/body/eval_jaxpr/all_gather | solution.py:77
  1302.1 14.4 %psum.15 = f32[2,32]{1,0:T(2,128)} all-reduce(f32[2,32]{1,0:T(2,128)S(1)} %convolution_bitcast_fusion.2), channel_id=1, replica_groups=mesh['section'=8,'tp'=16] {'section'}, use_global_device_ids=true, to_apply=%region_4.5 | all-reduce | flops 64 | bytes 512 | tf_op jit(solution)/shard_map/psum | solution.py:109
  (212 shorter events, 179.6 us)
Async XLA Ops:
  6.5 1295.3 %copy-start = (bf16[2,32,2048]{2,1,0:T(8,128)(2,1)S(1)}, bf16[2,32,2048]{2,1,0:T(8,128)(2,1)}, u32[]{:S(2)}) copy-start(bf16[2,32,2048]{2,1,0:T(8,128)(2,1)} %param.13) | copy-start | bytes 786436
  6.5 90.4 %all-reduce.2.cloned.1.call-start = ((), (), s32[]{:S(2)}) async-start(), calls=%async_computation | async-start | bytes 524288 | tf_op jit(solution)/shard_map/psum | solution.py:49
  8.8 89.2 %copy-start.3 = (bf16[2,256,32]{1,2,0:T(8,128)(2,1)S(1)}, bf16[2,256,32]{1,2,0:T(8,128)(2,1)}, u32[]{:S(2)}) copy-start(bf16[2,256,32]{1,2,0:T(8,128)(2,1)} %param.12) | copy-start | bytes 98308
  8.8 89.2 %copy-start.4 = (s32[4]{0:T(128)S(1)}, s32[4]{0:T(128)}, u32[]{:S(2)}) copy-start(s32[4]{0:T(128)} %param.15) | copy-start | bytes 52
  98.0 62.9 %all-gather.3.cloned.1.call-start = ((), (), s32[]{:S(2)}) async-start(), calls=%async_computation.1 | async-start | bytes 1114112 | tf_op jit(solution)/shard_map/while/body/eval_jaxpr/all_gather | solution.py:73
  98.0 17.6 %collective-permute-start = (bf16[128,4096]{1,0:T(8,128)(2,1)}, bf16[128,4096]{1,0:T(8,128)(2,1)S(1)}, u32[]{:S(2)}, u32[]{:S(2)}) collective-permute-start(bf16[128,4096]{1,0:T(8,128)(2,1)} %get-tuple-element.466), channel_id=1, source_target_pairs={{16,0},{32,16},{48,32},{64,48},{80,64},{96,80},{112,96},{17,1},{33... | collective-permute-start | bytes 3145736 | tf_op jit(solution)/shard_map/while/body/eval_jaxpr/ppermute | solution.py:15
  120.2 46.2 %copy-start.1 = (bf16[128,256]{1,0:T(8,128)(2,1)S(1)}, bf16[128,256]{1,0:T(8,128)(2,1)}, u32[]{:S(2)}) copy-start(bf16[128,256]{1,0:T(8,128)(2,1)} %add_convert_fusion.4) | copy-start | bytes 196612 | tf_op jit(solution)/shard_map/while
  120.2 87.2 %all-gather.5.cloned.1.call-start = ((), (), s32[]{:S(2)}) async-start(), calls=%async_computation.2 | async-start | bytes 1114112 | tf_op jit(solution)/shard_map/while/body/eval_jaxpr/all_gather | solution.py:77
  207.4 63.0 %all-gather.3.cloned.1.call-start = ((), (), s32[]{:S(2)}) async-start(), calls=%async_computation.1 | async-start | bytes 1114112 | tf_op jit(solution)/shard_map/while/body/eval_jaxpr/all_gather | solution.py:73
  207.4 17.7 %collective-permute-start = (bf16[128,4096]{1,0:T(8,128)(2,1)}, bf16[128,4096]{1,0:T(8,128)(2,1)S(1)}, u32[]{:S(2)}, u32[]{:S(2)}) collective-permute-start(bf16[128,4096]{1,0:T(8,128)(2,1)} %get-tuple-element.466), channel_id=1, source_target_pairs={{16,0},{32,16},{48,32},{64,48},{80,64},{96,80},{112,96},{17,1},{33... | collective-permute-start | bytes 3145736 | tf_op jit(solution)/shard_map/while/body/eval_jaxpr/ppermute | solution.py:15
  229.7 46.2 %copy-start.1 = (bf16[128,256]{1,0:T(8,128)(2,1)S(1)}, bf16[128,256]{1,0:T(8,128)(2,1)}, u32[]{:S(2)}) copy-start(bf16[128,256]{1,0:T(8,128)(2,1)} %add_convert_fusion.4) | copy-start | bytes 196612 | tf_op jit(solution)/shard_map/while
  229.7 87.2 %all-gather.5.cloned.1.call-start = ((), (), s32[]{:S(2)}) async-start(), calls=%async_computation.2 | async-start | bytes 1114112 | tf_op jit(solution)/shard_map/while/body/eval_jaxpr/all_gather | solution.py:77
  316.8 63.0 %all-gather.3.cloned.1.call-start = ((), (), s32[]{:S(2)}) async-start(), calls=%async_computation.1 | async-start | bytes 1114112 | tf_op jit(solution)/shard_map/while/body/eval_jaxpr/all_gather | solution.py:73
  316.8 17.7 %collective-permute-start = (bf16[128,4096]{1,0:T(8,128)(2,1)}, bf16[128,4096]{1,0:T(8,128)(2,1)S(1)}, u32[]{:S(2)}, u32[]{:S(2)}) collective-permute-start(bf16[128,4096]{1,0:T(8,128)(2,1)} %get-tuple-element.466), channel_id=1, source_target_pairs={{16,0},{32,16},{48,32},{64,48},{80,64},{96,80},{112,96},{17,1},{33... | collective-permute-start | bytes 3145736 | tf_op jit(solution)/shard_map/while/body/eval_jaxpr/ppermute | solution.py:15
  339.1 46.2 %copy-start.1 = (bf16[128,256]{1,0:T(8,128)(2,1)S(1)}, bf16[128,256]{1,0:T(8,128)(2,1)}, u32[]{:S(2)}) copy-start(bf16[128,256]{1,0:T(8,128)(2,1)} %add_convert_fusion.4) | copy-start | bytes 196612 | tf_op jit(solution)/shard_map/while
  339.1 87.2 %all-gather.5.cloned.1.call-start = ((), (), s32[]{:S(2)}) async-start(), calls=%async_computation.2 | async-start | bytes 1114112 | tf_op jit(solution)/shard_map/while/body/eval_jaxpr/all_gather | solution.py:77
  426.3 63.0 %all-gather.3.cloned.1.call-start = ((), (), s32[]{:S(2)}) async-start(), calls=%async_computation.1 | async-start | bytes 1114112 | tf_op jit(solution)/shard_map/while/body/eval_jaxpr/all_gather | solution.py:73
  426.3 17.7 %collective-permute-start = (bf16[128,4096]{1,0:T(8,128)(2,1)}, bf16[128,4096]{1,0:T(8,128)(2,1)S(1)}, u32[]{:S(2)}, u32[]{:S(2)}) collective-permute-start(bf16[128,4096]{1,0:T(8,128)(2,1)} %get-tuple-element.466), channel_id=1, source_target_pairs={{16,0},{32,16},{48,32},{64,48},{80,64},{96,80},{112,96},{17,1},{33... | collective-permute-start | bytes 3145736 | tf_op jit(solution)/shard_map/while/body/eval_jaxpr/ppermute | solution.py:15
  448.5 46.2 %copy-start.1 = (bf16[128,256]{1,0:T(8,128)(2,1)S(1)}, bf16[128,256]{1,0:T(8,128)(2,1)}, u32[]{:S(2)}) copy-start(bf16[128,256]{1,0:T(8,128)(2,1)} %add_convert_fusion.4) | copy-start | bytes 196612 | tf_op jit(solution)/shard_map/while
  448.5 87.2 %all-gather.5.cloned.1.call-start = ((), (), s32[]{:S(2)}) async-start(), calls=%async_computation.2 | async-start | bytes 1114112 | tf_op jit(solution)/shard_map/while/body/eval_jaxpr/all_gather | solution.py:77
  535.7 63.0 %all-gather.3.cloned.1.call-start = ((), (), s32[]{:S(2)}) async-start(), calls=%async_computation.1 | async-start | bytes 1114112 | tf_op jit(solution)/shard_map/while/body/eval_jaxpr/all_gather | solution.py:73
  535.7 17.7 %collective-permute-start = (bf16[128,4096]{1,0:T(8,128)(2,1)}, bf16[128,4096]{1,0:T(8,128)(2,1)S(1)}, u32[]{:S(2)}, u32[]{:S(2)}) collective-permute-start(bf16[128,4096]{1,0:T(8,128)(2,1)} %get-tuple-element.466), channel_id=1, source_target_pairs={{16,0},{32,16},{48,32},{64,48},{80,64},{96,80},{112,96},{17,1},{33... | collective-permute-start | bytes 3145736 | tf_op jit(solution)/shard_map/while/body/eval_jaxpr/ppermute | solution.py:15
  558.0 46.2 %copy-start.1 = (bf16[128,256]{1,0:T(8,128)(2,1)S(1)}, bf16[128,256]{1,0:T(8,128)(2,1)}, u32[]{:S(2)}) copy-start(bf16[128,256]{1,0:T(8,128)(2,1)} %add_convert_fusion.4) | copy-start | bytes 196612 | tf_op jit(solution)/shard_map/while
  558.0 87.2 %all-gather.5.cloned.1.call-start = ((), (), s32[]{:S(2)}) async-start(), calls=%async_computation.2 | async-start | bytes 1114112 | tf_op jit(solution)/shard_map/while/body/eval_jaxpr/all_gather | solution.py:77
  645.2 63.0 %all-gather.3.cloned.1.call-start = ((), (), s32[]{:S(2)}) async-start(), calls=%async_computation.1 | async-start | bytes 1114112 | tf_op jit(solution)/shard_map/while/body/eval_jaxpr/all_gather | solution.py:73
  645.2 17.7 %collective-permute-start = (bf16[128,4096]{1,0:T(8,128)(2,1)}, bf16[128,4096]{1,0:T(8,128)(2,1)S(1)}, u32[]{:S(2)}, u32[]{:S(2)}) collective-permute-start(bf16[128,4096]{1,0:T(8,128)(2,1)} %get-tuple-element.466), channel_id=1, source_target_pairs={{16,0},{32,16},{48,32},{64,48},{80,64},{96,80},{112,96},{17,1},{33... | collective-permute-start | bytes 3145736 | tf_op jit(solution)/shard_map/while/body/eval_jaxpr/ppermute | solution.py:15
  667.4 46.2 %copy-start.1 = (bf16[128,256]{1,0:T(8,128)(2,1)S(1)}, bf16[128,256]{1,0:T(8,128)(2,1)}, u32[]{:S(2)}) copy-start(bf16[128,256]{1,0:T(8,128)(2,1)} %add_convert_fusion.4) | copy-start | bytes 196612 | tf_op jit(solution)/shard_map/while
  667.4 87.2 %all-gather.5.cloned.1.call-start = ((), (), s32[]{:S(2)}) async-start(), calls=%async_computation.2 | async-start | bytes 1114112 | tf_op jit(solution)/shard_map/while/body/eval_jaxpr/all_gather | solution.py:77
  754.6 63.0 %all-gather.3.cloned.1.call-start = ((), (), s32[]{:S(2)}) async-start(), calls=%async_computation.1 | async-start | bytes 1114112 | tf_op jit(solution)/shard_map/while/body/eval_jaxpr/all_gather | solution.py:73
  754.6 17.7 %collective-permute-start = (bf16[128,4096]{1,0:T(8,128)(2,1)}, bf16[128,4096]{1,0:T(8,128)(2,1)S(1)}, u32[]{:S(2)}, u32[]{:S(2)}) collective-permute-start(bf16[128,4096]{1,0:T(8,128)(2,1)} %get-tuple-element.466), channel_id=1, source_target_pairs={{16,0},{32,16},{48,32},{64,48},{80,64},{96,80},{112,96},{17,1},{33... | collective-permute-start | bytes 3145736 | tf_op jit(solution)/shard_map/while/body/eval_jaxpr/ppermute | solution.py:15
  776.8 46.2 %copy-start.1 = (bf16[128,256]{1,0:T(8,128)(2,1)S(1)}, bf16[128,256]{1,0:T(8,128)(2,1)}, u32[]{:S(2)}) copy-start(bf16[128,256]{1,0:T(8,128)(2,1)} %add_convert_fusion.4) | copy-start | bytes 196612 | tf_op jit(solution)/shard_map/while
  776.9 87.2 %all-gather.5.cloned.1.call-start = ((), (), s32[]{:S(2)}) async-start(), calls=%async_computation.2 | async-start | bytes 1114112 | tf_op jit(solution)/shard_map/while/body/eval_jaxpr/all_gather | solution.py:77
  864.0 63.0 %all-gather.3.cloned.1.call-start = ((), (), s32[]{:S(2)}) async-start(), calls=%async_computation.1 | async-start | bytes 1114112 | tf_op jit(solution)/shard_map/while/body/eval_jaxpr/all_gather | solution.py:73
  864.0 17.7 %collective-permute-start = (bf16[128,4096]{1,0:T(8,128)(2,1)}, bf16[128,4096]{1,0:T(8,128)(2,1)S(1)}, u32[]{:S(2)}, u32[]{:S(2)}) collective-permute-start(bf16[128,4096]{1,0:T(8,128)(2,1)} %get-tuple-element.466), channel_id=1, source_target_pairs={{16,0},{32,16},{48,32},{64,48},{80,64},{96,80},{112,96},{17,1},{33... | collective-permute-start | bytes 3145736 | tf_op jit(solution)/shard_map/while/body/eval_jaxpr/ppermute | solution.py:15
  886.3 46.2 %copy-start.1 = (bf16[128,256]{1,0:T(8,128)(2,1)S(1)}, bf16[128,256]{1,0:T(8,128)(2,1)}, u32[]{:S(2)}) copy-start(bf16[128,256]{1,0:T(8,128)(2,1)} %add_convert_fusion.4) | copy-start | bytes 196612 | tf_op jit(solution)/shard_map/while
  886.3 87.2 %all-gather.5.cloned.1.call-start = ((), (), s32[]{:S(2)}) async-start(), calls=%async_computation.2 | async-start | bytes 1114112 | tf_op jit(solution)/shard_map/while/body/eval_jaxpr/all_gather | solution.py:77
  973.5 63.0 %all-gather.3.cloned.1.call-start = ((), (), s32[]{:S(2)}) async-start(), calls=%async_computation.1 | async-start | bytes 1114112 | tf_op jit(solution)/shard_map/while/body/eval_jaxpr/all_gather | solution.py:73
  973.5 17.7 %collective-permute-start = (bf16[128,4096]{1,0:T(8,128)(2,1)}, bf16[128,4096]{1,0:T(8,128)(2,1)S(1)}, u32[]{:S(2)}, u32[]{:S(2)}) collective-permute-start(bf16[128,4096]{1,0:T(8,128)(2,1)} %get-tuple-element.466), channel_id=1, source_target_pairs={{16,0},{32,16},{48,32},{64,48},{80,64},{96,80},{112,96},{17,1},{33... | collective-permute-start | bytes 3145736 | tf_op jit(solution)/shard_map/while/body/eval_jaxpr/ppermute | solution.py:15
  995.7 46.2 %copy-start.1 = (bf16[128,256]{1,0:T(8,128)(2,1)S(1)}, bf16[128,256]{1,0:T(8,128)(2,1)}, u32[]{:S(2)}) copy-start(bf16[128,256]{1,0:T(8,128)(2,1)} %add_convert_fusion.4) | copy-start | bytes 196612 | tf_op jit(solution)/shard_map/while
  995.7 87.2 %all-gather.5.cloned.1.call-start = ((), (), s32[]{:S(2)}) async-start(), calls=%async_computation.2 | async-start | bytes 1114112 | tf_op jit(solution)/shard_map/while/body/eval_jaxpr/all_gather | solution.py:77
  1082.9 63.0 %all-gather.3.cloned.1.call-start = ((), (), s32[]{:S(2)}) async-start(), calls=%async_computation.1 | async-start | bytes 1114112 | tf_op jit(solution)/shard_map/while/body/eval_jaxpr/all_gather | solution.py:73
  1082.9 17.7 %collective-permute-start = (bf16[128,4096]{1,0:T(8,128)(2,1)}, bf16[128,4096]{1,0:T(8,128)(2,1)S(1)}, u32[]{:S(2)}, u32[]{:S(2)}) collective-permute-start(bf16[128,4096]{1,0:T(8,128)(2,1)} %get-tuple-element.466), channel_id=1, source_target_pairs={{16,0},{32,16},{48,32},{64,48},{80,64},{96,80},{112,96},{17,1},{33... | collective-permute-start | bytes 3145736 | tf_op jit(solution)/shard_map/while/body/eval_jaxpr/ppermute | solution.py:15
  1105.2 46.2 %copy-start.1 = (bf16[128,256]{1,0:T(8,128)(2,1)S(1)}, bf16[128,256]{1,0:T(8,128)(2,1)}, u32[]{:S(2)}) copy-start(bf16[128,256]{1,0:T(8,128)(2,1)} %add_convert_fusion.4) | copy-start | bytes 196612 | tf_op jit(solution)/shard_map/while
  1105.2 87.2 %all-gather.5.cloned.1.call-start = ((), (), s32[]{:S(2)}) async-start(), calls=%async_computation.2 | async-start | bytes 1114112 | tf_op jit(solution)/shard_map/while/body/eval_jaxpr/all_gather | solution.py:77
  1192.4 63.0 %all-gather.3.cloned.1.call-start = ((), (), s32[]{:S(2)}) async-start(), calls=%async_computation.1 | async-start | bytes 1114112 | tf_op jit(solution)/shard_map/while/body/eval_jaxpr/all_gather | solution.py:73
  1192.4 17.7 %collective-permute-start = (bf16[128,4096]{1,0:T(8,128)(2,1)}, bf16[128,4096]{1,0:T(8,128)(2,1)S(1)}, u32[]{:S(2)}, u32[]{:S(2)}) collective-permute-start(bf16[128,4096]{1,0:T(8,128)(2,1)} %get-tuple-element.466), channel_id=1, source_target_pairs={{16,0},{32,16},{48,32},{64,48},{80,64},{96,80},{112,96},{17,1},{33... | collective-permute-start | bytes 3145736 | tf_op jit(solution)/shard_map/while/body/eval_jaxpr/ppermute | solution.py:15
  1214.6 46.2 %copy-start.1 = (bf16[128,256]{1,0:T(8,128)(2,1)S(1)}, bf16[128,256]{1,0:T(8,128)(2,1)}, u32[]{:S(2)}) copy-start(bf16[128,256]{1,0:T(8,128)(2,1)} %add_convert_fusion.4) | copy-start | bytes 196612 | tf_op jit(solution)/shard_map/while
  1214.6 87.2 %all-gather.5.cloned.1.call-start = ((), (), s32[]{:S(2)}) async-start(), calls=%async_computation.2 | async-start | bytes 1114112 | tf_op jit(solution)/shard_map/while/body/eval_jaxpr/all_gather | solution.py:77
  (1 other events, 2.3 us)
Sparse Core Ops, SparseCore 0:
  10.5 86.3 all-reduce.1
  120.3 40.5 all-gather.2
  164.4 42.9 all-gather.4
  229.8 40.5 all-gather.2
  273.8 42.9 all-gather.4
  339.2 40.5 all-gather.2
  383.3 42.9 all-gather.4
  448.6 40.5 all-gather.2
  492.7 42.9 all-gather.4
  558.1 40.5 all-gather.2
  602.1 42.9 all-gather.4
  667.5 40.5 all-gather.2
  711.6 42.9 all-gather.4
  777.0 40.5 all-gather.2
  821.0 42.9 all-gather.4
  886.4 40.5 all-gather.2
  930.5 42.9 all-gather.4
  995.8 40.5 all-gather.2
  1039.9 42.9 all-gather.4
  1105.3 40.5 all-gather.2
  1149.3 42.9 all-gather.4
  1214.7 40.5 all-gather.2
  1258.8 42.9 all-gather.4
